TPU v7x, 256 devices: a whole 4x4x8 slice. The times are simulated.
256 devices in a mesh: lon: 16 (over z, y_lo), lat: 8 (over x, y_hi), lev: 2 (over core).
Axes of the slice: x: 4, y: 4 (y_hi: 2, y_lo: 2; y = y_hi * 2 + y_lo), z: 8, core: 2. Of those that a mesh axis runs over, the one named last changes fastest.
Arguments:
- adjoint_in: float32 [9, 16, 128, 2048], P(None, 'lev', 'lat', 'lon'), may hold values from -6 to 6
- trajectory: bfloat16 [3, 9, 16, 128, 2048], P(None, None, 'lev', 'lat', 'lon'), may hold values from 0.5 to 2
- courant: float32 [2, 16, 128, 2048], P(None, 'lev', 'lat', 'lon'), may hold values from -0.4 to 0.4
- mixing: float32 [16, 128, 2048], P('lev', 'lat', 'lon'), may hold values from 0.02 to 0.2
- coag_rates: float32 [6, 16], replicated, may hold values from 0.02 to 0.2
- settle_speed: float32 [8, 9], replicated, may hold values from 0.01 to 0.2
- settle_class: int32 [16], replicated, may hold values from 0 to 7
- emis_profile: float32 [16], replicated, may hold values from 0.1 to 1
- emis_coef: float32 [9], replicated, may hold values from 0.5 to 2
- land_mask: int32 [128, 2048], P('lat', 'lon'), may hold values 0 or 1
- source_mask: int32 [128, 2048], P('lat', 'lon'), may hold values 0 or 1
Outputs:
- adjoint_out: float32 [9, 16, 128, 2048], P(None, 'lev', 'lat', 'lon')
- emis_grad: float32 [3, 128, 2048], P(None, 'lat', 'lon')
All inputs are finite; a program needn't handle non-finite values. No bound on the sum of `land_mask` or of `source_mask` on one device may be relied on, other than what follows from the above.
Results may differ from a plain program's by a relative error of at most 0.0003.
Values may be sent and summed in bfloat16 or wider, within the bound.
A program may use at most 64 MiB of HBM per device.

v0:
```python
import jax
import jax.numpy as jnp
from jax import lax
from jax.sharding import PartitionSpec as P


def with_halo(cells, sides, width, closed):
    for axis, dim in sides:
        count = lax.axis_size(axis)
        ends = count if closed else count - 1
        head = lax.slice_in_dim(cells, 0, width, axis=dim)
        tail = lax.slice_in_dim(cells, cells.shape[dim] - width, cells.shape[dim], axis=dim)
        cells = jnp.concatenate(
            [
                lax.ppermute(tail, axis, [(i, (i + 1) % count) for i in range(ends)]),
                cells,
                lax.ppermute(head, axis, [((i + 1) % count, i) for i in range(ends)]),
            ],
            axis=dim,
        )
    return cells


def slab(field, axis, start, length):
    return lax.slice_in_dim(field, start, start + length, axis=axis)


def transport(padded, courant_pad, axis, length):
    courant_wide = courant_pad[None]
    diff_face = slab(padded, axis, 0, length + 3) - slab(padded, axis, 1, length + 3)
    face_speed = slab(courant_wide, axis, 0, length + 3)
    forward_part = jnp.maximum(face_speed, 0.0) * diff_face
    backward_part = jnp.minimum(face_speed, 0.0) * diff_face
    return (
        -1.5 * slab(forward_part, axis, 2, length)
        + 0.5 * slab(forward_part, axis, 3, length)
        - 1.5 * slab(backward_part, axis, 1, length)
        + 0.5 * slab(backward_part, axis, 0, length)
    )


def vertical(padded, mixing_pad, speeds, deposit):
    depth_count = padded.shape[1] - 2
    mixing_below = mixing_pad[:depth_count]
    mixing_above = mixing_pad[1 : depth_count + 1]
    speed_level = speeds[:, :, None, None]
    centre = padded[:, 1 : depth_count + 1]
    return (
        centre * (1.0 - mixing_above - mixing_below - speed_level - deposit)
        + padded[:, :depth_count] * (mixing_below + speed_level)
        + padded[:, 2:] * mixing_above
    )


def coag_increment(state, rates):
    rate_grid = rates[:, :, None, None]
    number = [state[0], state[3], state[6]]
    volume = [state[1], state[4], state[7]]
    moment_six = [state[2], state[5], state[8]]
    pair_rate = {(0, 1): rate_grid[3], (0, 2): rate_grid[4], (1, 2): rate_grid[5]}
    outputs = []
    for mode_index in range(3):
        d_number = -rate_grid[mode_index] * number[mode_index] * number[mode_index]
        d_volume = jnp.zeros_like(number[mode_index])
        d_moment = rate_grid[mode_index] * volume[mode_index] * volume[mode_index]
        for other_mode in range(3):
            if other_mode > mode_index:
                pair = pair_rate[mode_index, other_mode]
                d_number = d_number - pair * number[mode_index] * number[other_mode]
                d_volume = d_volume - pair * volume[mode_index] * number[other_mode]
                d_moment = d_moment - pair * moment_six[mode_index] * number[other_mode]
            if other_mode < mode_index:
                pair = pair_rate[other_mode, mode_index]
                d_volume = d_volume + pair * volume[other_mode] * number[mode_index]
                d_moment = d_moment + pair * (
                    moment_six[other_mode] * number[mode_index]
                    + 2.0 * volume[other_mode] * volume[mode_index]
                )
        outputs.extend([d_number, d_volume, d_moment])
    return jnp.stack(outputs)


def coag_adjoint(adjoint, state, rates):
    primal_out, pullback = jax.vjp(lambda value: coag_increment(value, rates), state)
    return adjoint + pullback(adjoint)[0]


def emission_part(adjoint, profile, emis_coef, source):
    weighted = adjoint * (emis_coef[:, None, None, None] * profile[None, :, None, None])
    per_tracer = jnp.sum(weighted, axis=1)
    per_mode = jnp.sum(per_tracer.reshape(3, 3, per_tracer.shape[1], per_tracer.shape[2]), axis=1)
    return per_mode * source


def sides(field, lat_index, row_count, lat_count):
    lon_pad = with_halo(field, (("lon", 3),), 2, True)
    lat_pad = with_halo(field, (("lat", 2),), 2, False)
    return (lon_pad, lat_pad)


def planes(field):
    return with_halo(field, (("lev", 1),), 1, False)


def run_split(
    adjoint_in,
    trajectory,
    winds,
    mixing_top,
    coag_rates,
    speeds_all,
    emis_profile,
    emis_coef,
    dep_rows,
    source,
):
    depth_count = adjoint_in.shape[1]
    row_count = adjoint_in.shape[2]
    col_count = adjoint_in.shape[3]
    lev_index = lax.axis_index("lev")
    lat_index = lax.axis_index("lat")
    lat_count = lax.axis_size("lat")
    level_global = lev_index * depth_count + jnp.arange(depth_count, dtype=jnp.int32)
    level_start = lev_index * depth_count
    rates_own = lax.dynamic_slice_in_dim(coag_rates, level_start, depth_count, 1)
    profile_own = lax.dynamic_slice_in_dim(emis_profile, level_start, depth_count, 0)
    wind_lon, wind_lat = sides(winds, lat_index, row_count, lat_count)
    east_pad = wind_lon[0]
    north_pad = wind_lat[1]
    mixing_pad = planes(mixing_top[None])[0]
    speeds_used = lax.dynamic_slice_in_dim(speeds_all, level_start, depth_count, 1)
    surface = (level_global == 0).astype(jnp.float32)
    deposit = dep_rows[None] * surface[:, None, None]
    adjoint = adjoint_in
    emis_grad = jnp.zeros((3, row_count, col_count), jnp.float32)
    for step_index in range(trajectory.shape[0] - 1, -1, -1):
        emis_grad = emis_grad + emission_part(adjoint, profile_own, emis_coef, source)
        adjoint = coag_adjoint(adjoint, trajectory[step_index].astype(jnp.float32), rates_own)
        adjoint = vertical(planes(adjoint), mixing_pad, speeds_used, deposit)
        lon_pad, lat_pad = sides(adjoint, lat_index, row_count, lat_count)
        adjoint = (
            adjoint
            + transport(lon_pad, east_pad, 3, col_count)
            + transport(lat_pad, north_pad, 2, row_count)
        )
    emis_grad = lax.psum(emis_grad, "lev")
    return (adjoint, emis_grad)


def shards(
    adjoint_in,
    trajectory,
    courant,
    mixing,
    coag_rates,
    settle_speed,
    settle_class,
    emis_profile,
    emis_coef,
    land_mask,
    source_mask,
):
    depth_count = adjoint_in.shape[1]
    row_count = adjoint_in.shape[2]
    lev_index = lax.axis_index("lev")
    lat_index = lax.axis_index("lat")
    lat_count = lax.axis_size("lat")
    level_total = settle_class.shape[0]
    row_global = lat_index * row_count + jnp.arange(row_count, dtype=jnp.int32)
    top_row = (row_global == row_count * lat_count - 1)[None, :, None]
    winds = jnp.stack([courant[0], jnp.where(top_row, 0.0, courant[1])])
    level_global = lev_index * depth_count + jnp.arange(depth_count, dtype=jnp.int32)
    mixing_top = jnp.where((level_global == level_total - 1)[:, None, None], 0.0, mixing)
    choose = (
        settle_class[:, None] == jnp.arange(settle_speed.shape[0], dtype=jnp.int32)[None, :]
    ).astype(jnp.float32)
    speeds_all = jnp.dot(choose, settle_speed, precision=lax.Precision.HIGHEST).T
    dep_rows = 0.1 + 0.3 * land_mask.astype(jnp.float32)
    source = source_mask.astype(jnp.float32)
    return run_split(
        adjoint_in,
        trajectory,
        winds,
        mixing_top,
        coag_rates,
        speeds_all,
        emis_profile,
        emis_coef,
        dep_rows,
        source,
    )


def solution(mesh):
    return jax.shard_map(
        shards,
        mesh=mesh,
        in_specs=(
            P(None, "lev", "lat", "lon"),
            P(None, None, "lev", "lat", "lon"),
            P(None, "lev", "lat", "lon"),
            P("lev", "lat", "lon"),
            P(),
            P(),
            P(),
            P(),
            P(),
            P("lat", "lon"),
            P("lat", "lon"),
        ),
        out_specs=(P(None, "lev", "lat", "lon"), P(None, "lat", "lon")),
        check_vma=False,
    )
```

profile of v0, /device:TPU:6, one launch (start us, length us, event | category | flops | bytes accessed | tf_op | source)
XLA Modules:
  0.0 130.4 jit_solution(11100671563132194854)
XLA Ops:
  0.7 0.8 constant_dynamic-slice_fusion
  1.5 1.4 %slice_convert_fusion = (f32[1,9,8,16,128]{4,3,2,1,0:T(8,128)S(1)}, f32[1,9,8,16,128]{4,3,2,1,0:T(8,128)S(1)}, f32[1,9,8,16,128]{4,3,2,1,0:T(8,128)S(1)}) fusion(bf16[3,9,8,16,128]{4,3,2,1,0:T(8,128)(2,1)} %param.12), kind=kLoop, calls=%fused_computation.97 | loop fusion | flops 442368 | bytes 2654208 | tf_op jit(solution)/shard_map/convert_element_type | solution.py:138
  4.4 1.7 %collective-permute-start.1 = (f32[9,1,16,128]{3,2,1,0:T(8,128)}, f32[9,1,16,128]{3,2,1,0:T(8,128)S(1)}, u32[]{:S(2)}, u32[]{:S(2)}) collective-permute-start(f32[9,1,16,128]{3,2,1,0:T(8,128)} %get-tuple-element.54), channel_id=1, source_target_pairs={{0,1},{2,3},{4,5},{6,7},{8,9},{10,11},{12,13},{14,15},{16,17},{18,... | collective-permute-start | bytes 221192 | tf_op jit(solution)/shard_map/ppermute | solution.py:15
  6.2 1.3 collective-permute-start.2
  7.6 3.0 %collective-permute-start = (f32[1,1,16,128]{3,2,1,0:T(8,128)S(1)}, f32[1,1,16,128]{3,2,1,0:T(8,128)S(1)}, u32[]{:S(2)}, u32[]{:S(2)}) collective-permute-start(f32[1,1,16,128]{3,2,1,0:T(8,128)S(1)} %slice.569), channel_id=1, source_target_pairs={{0,1},{2,3},{4,5},{6,7},{8,9},{10,11},{12,13},{14,15},{16,17},{18,... | collective-permute-start | bytes 24584 | tf_op jit(solution)/shard_map/ppermute | solution.py:15
  10.8 1.7 %collective-permute-start.3 = (f32[2,8,16,2]{3,2,1,0:T(8,128)S(1)}, f32[2,8,16,2]{3,2,1,0:T(8,128)S(1)}, u32[]{:S(2)}, u32[]{:S(2)}) collective-permute-start(f32[2,8,16,2]{3,2,1,0:T(8,128)S(1)} %get-tuple-element.60), channel_id=1, source_target_pairs={{0,16},{16,32},{32,48},{48,64},{64,80},{80,96},{96,112},{112,128},... | collective-permute-start | bytes 6152 | tf_op jit(solution)/shard_map/ppermute | solution.py:15
  12.5 5.4 %collective-permute-start.4 = (f32[2,8,16,2]{3,2,1,0:T(8,128)S(1)}, f32[2,8,16,2]{3,2,1,0:T(8,128)S(1)}, u32[]{:S(2)}, u32[]{:S(2)}) collective-permute-start(f32[2,8,16,2]{3,2,1,0:T(8,128)S(1)} %get-tuple-element.61), channel_id=1, source_target_pairs={{16,0},{32,16},{48,32},{64,48},{80,64},{96,80},{112,96},{128,112},... | collective-permute-start | bytes 6152 | tf_op jit(solution)/shard_map/ppermute | solution.py:17
  19.0 1.8 %collective-permute-done.3 = f32[2,8,16,2]{3,2,1,0:T(8,128)S(1)} collective-permute-done((f32[2,8,16,2]{3,2,1,0:T(8,128)S(1)}, f32[2,8,16,2]{3,2,1,0:T(8,128)S(1)}, u32[]{:S(2)}, u32[]{:S(2)}) %collective-permute-start.3) | collective-permute-done | bytes 2080 | tf_op jit(solution)/shard_map/ppermute | solution.py:15
  20.8 4.9 %collective-permute-start.7 = (f32[2,8,2,128]{3,2,1,0:T(2,128)S(1)}, f32[2,8,2,128]{3,2,1,0:T(2,128)S(1)}, u32[]{:S(2)}, u32[]{:S(2)}) collective-permute-start(f32[2,8,2,128]{3,2,1,0:T(2,128)S(1)} %get-tuple-element.62), channel_id=1, source_target_pairs={{0,2},{2,4},{4,6},{6,8},{8,10},{10,12},{12,14},{1,3},{3,5},{5,7},{... | collective-permute-start | bytes 49160 | tf_op jit(solution)/shard_map/ppermute | solution.py:15
  25.8 3.3 %collective-permute-start.8 = (f32[2,8,2,128]{3,2,1,0:T(2,128)S(1)}, f32[2,8,2,128]{3,2,1,0:T(2,128)S(1)}, u32[]{:S(2)}, u32[]{:S(2)}) collective-permute-start(f32[2,8,2,128]{3,2,1,0:T(2,128)S(1)} %get-tuple-element.63), channel_id=1, source_target_pairs={{2,0},{4,2},{6,4},{8,6},{10,8},{12,10},{14,12},{3,1},{5,3},{7,5},{... | collective-permute-start | bytes 49160 | tf_op jit(solution)/shard_map/ppermute | solution.py:17
  29.2 0.7 fusion.35
  30.0 2.9 %collective-permute-done.8 = f32[2,8,2,128]{3,2,1,0:T(2,128)S(1)} collective-permute-done((f32[2,8,2,128]{3,2,1,0:T(2,128)S(1)}, f32[2,8,2,128]{3,2,1,0:T(2,128)S(1)}, u32[]{:S(2)}, u32[]{:S(2)}) %collective-permute-start.8) | collective-permute-done | bytes 16416 | tf_op jit(solution)/shard_map/ppermute | solution.py:17
  34.3 1.1 fusion.1
  35.5 1.2 fusion.57
  36.6 2.2 %copy.101 = f32[9,8,16,2]{2,1,3,0:T(8,128)} copy(f32[9,8,16,2]{3,2,1,0:T(8,128)} %get-tuple-element.50) | data formatting | bytes 18432 | tf_op jit(solution)/shard_map/slice | solution.py:12
  38.8 2.2 %copy.102 = f32[9,8,16,2]{2,1,3,0:T(8,128)} copy(f32[9,8,16,2]{3,2,1,0:T(8,128)} %get-tuple-element.51) | data formatting | bytes 18432 | tf_op jit(solution)/shard_map/slice | solution.py:11
  41.0 4.1 %collective-permute-start.6 = (f32[9,8,16,2]{2,1,3,0:T(8,128)}, f32[9,8,16,2]{2,1,3,0:T(8,128)}, u32[]{:S(2)}, u32[]{:S(2)}) collective-permute-start(f32[9,8,16,2]{2,1,3,0:T(8,128)} %copy.102), channel_id=1, source_target_pairs={{16,0},{32,16},{48,32},{64,48},{80,64},{96,80},{112,96},{128,112},... | collective-permute-start | bytes 27656 | tf_op jit(solution)/shard_map/ppermute | solution.py:17
  45.8 2.0 %collective-permute-start.9 = (f32[9,8,2,128]{3,1,2,0:T(8,128)}, f32[9,8,2,128]{3,1,2,0:T(8,128)}, u32[]{:S(2)}, u32[]{:S(2)}) collective-permute-start(f32[9,8,2,128]{3,1,2,0:T(8,128)} %copy.105), channel_id=1, source_target_pairs={{0,2},{2,4},{4,6},{6,8},{8,10},{10,12},{12,14},{1,3},{3,5},{5,7},{... | collective-permute-start | bytes 221192 | tf_op jit(solution)/shard_map/ppermute | solution.py:15
  48.5 6.2 %collective-permute-start.10 = (f32[9,8,2,128]{3,1,2,0:T(8,128)}, f32[9,8,2,128]{3,1,2,0:T(8,128)}, u32[]{:S(2)}, u32[]{:S(2)}) collective-permute-start(f32[9,8,2,128]{3,1,2,0:T(8,128)} %copy.106), channel_id=1, source_target_pairs={{2,0},{4,2},{6,4},{8,6},{10,8},{12,10},{14,12},{3,1},{5,3},{7,5},{... | collective-permute-start | bytes 221192 | tf_op jit(solution)/shard_map/ppermute | solution.py:17
  54.7 2.2 %copy.103 = f32[9,8,16,2]{3,2,1,0:T(8,128)} copy(f32[9,8,16,2]{2,1,3,0:T(8,128)} %collective-permute-done.5) | data formatting | bytes 18432 | tf_op jit(solution)/shard_map/ppermute | solution.py:15
  56.9 2.2 %copy.104 = f32[9,8,16,2]{3,2,1,0:T(8,128)} copy(f32[9,8,16,2]{2,1,3,0:T(8,128)} %collective-permute-done.6) | data formatting | bytes 18432 | tf_op jit(solution)/shard_map/ppermute | solution.py:17
  59.1 1.8 %pad_maximum_fusion = f32[9,8,16,132]{3,2,1,0:T(8,128)S(1)} fusion(f32[9,8,16,2]{3,2,1,0:T(8,128)} %copy.104, f32[9,8,16,128]{3,2,1,0:T(8,128)S(1)} %fusion.1, f32[9,8,16,2]{3,2,1,0:T(8,128)} %copy.103), kind=kLoop, calls=%fused_computation.3 | loop fusion | flops 304128 | bytes 1216512 | tf_op jit(solution)/shard_map/concatenate | solution.py:13
  61.4 1.0 copy.107
  62.4 0.9 copy.108
  64.4 0.7 fusion.25
  66.3 1.3 collective-permute-start.11
  67.6 1.3 collective-permute-start.12
  69.0 1.7 %collective-permute-done.12 = f32[9,1,16,128]{3,2,1,0:T(8,128)S(1)} collective-permute-done((f32[9,1,16,128]{3,2,1,0:T(8,128)S(1)}, f32[9,1,16,128]{3,2,1,0:T(8,128)S(1)}, u32[]{:S(2)}, u32[]{:S(2)}) %collective-permute-start.12) | collective-permute-done | bytes 73760 | tf_op jit(solution)/shard_map/ppermute | solution.py:17
  71.0 1.2 fusion.54
  72.2 2.2 %copy.109 = f32[9,8,16,2]{2,1,3,0:T(8,128)} copy(f32[9,8,16,2]{3,2,1,0:T(8,128)} %get-tuple-element.44) | data formatting | bytes 18432 | tf_op jit(solution)/shard_map/slice | solution.py:12
  74.4 2.2 %copy.110 = f32[9,8,16,2]{2,1,3,0:T(8,128)} copy(f32[9,8,16,2]{3,2,1,0:T(8,128)} %get-tuple-element.45) | data formatting | bytes 18432 | tf_op jit(solution)/shard_map/slice | solution.py:11
  76.6 4.1 %collective-permute-start.14 = (f32[9,8,16,2]{2,1,3,0:T(8,128)}, f32[9,8,16,2]{2,1,3,0:T(8,128)}, u32[]{:S(2)}, u32[]{:S(2)}) collective-permute-start(f32[9,8,16,2]{2,1,3,0:T(8,128)} %copy.110), channel_id=1, source_target_pairs={{16,0},{32,16},{48,32},{64,48},{80,64},{96,80},{112,96},{128,112},... | collective-permute-start | bytes 27656 | tf_op jit(solution)/shard_map/ppermute | solution.py:17
  81.4 1.9 %collective-permute-start.15 = (f32[9,8,2,128]{3,1,2,0:T(8,128)}, f32[9,8,2,128]{3,1,2,0:T(8,128)}, u32[]{:S(2)}, u32[]{:S(2)}) collective-permute-start(f32[9,8,2,128]{3,1,2,0:T(8,128)} %copy.113), channel_id=1, source_target_pairs={{0,2},{2,4},{4,6},{6,8},{8,10},{10,12},{12,14},{1,3},{3,5},{5,7},{... | collective-permute-start | bytes 221192 | tf_op jit(solution)/shard_map/ppermute | solution.py:15
  84.0 6.5 %collective-permute-start.16 = (f32[9,8,2,128]{3,1,2,0:T(8,128)}, f32[9,8,2,128]{3,1,2,0:T(8,128)}, u32[]{:S(2)}, u32[]{:S(2)}) collective-permute-start(f32[9,8,2,128]{3,1,2,0:T(8,128)} %copy.114), channel_id=1, source_target_pairs={{2,0},{4,2},{6,4},{8,6},{10,8},{12,10},{14,12},{3,1},{5,3},{7,5},{... | collective-permute-start | bytes 221192 | tf_op jit(solution)/shard_map/ppermute | solution.py:17
  90.5 2.2 %copy.111 = f32[9,8,16,2]{3,2,1,0:T(8,128)} copy(f32[9,8,16,2]{2,1,3,0:T(8,128)} %collective-permute-done.13) | data formatting | bytes 18432 | tf_op jit(solution)/shard_map/ppermute | solution.py:15
  92.7 2.2 %copy.112 = f32[9,8,16,2]{3,2,1,0:T(8,128)} copy(f32[9,8,16,2]{2,1,3,0:T(8,128)} %collective-permute-done.14) | data formatting | bytes 18432 | tf_op jit(solution)/shard_map/ppermute | solution.py:17
  94.9 1.8 %pad_maximum_fusion.1 = f32[9,8,16,132]{3,2,1,0:T(8,128)S(1)} fusion(f32[9,8,16,2]{3,2,1,0:T(8,128)} %copy.112, f32[9,8,16,128]{3,2,1,0:T(8,128)S(1)} %fusion.3, f32[9,8,16,2]{3,2,1,0:T(8,128)} %copy.111), kind=kLoop, calls=%fused_computation.4 | loop fusion | flops 304128 | bytes 1216512 | tf_op jit(solution)/shard_map/concatenate | solution.py:13
  97.2 1.0 copy.115
  98.2 0.9 copy.116
  100.2 1.6 %multiply_reduce_fusion.1 = (f32[9,16,128]{2,1,0:T(8,128)}, f32[9,16,128]{2,1,0:T(8,128)}, f32[9,16,128]{2,1,0:T(8,128)}, f32[9,8,16,128]{3,2,1,0:T(8,128)S(1)}) fusion(f32[9,8,16,128]{3,2,1,0:T(8,128)S(1)} %fusion.25, f32[9,8]{1,0:T(8,128)S(1)} %broadcast_multiply_fusion.13, f32[9,8,16,128]{3,2,1,0:T(8,128)S(1)} %copy-done.1, ...), kind=kLoop, calls=%fused_computation.79 | loop fusion | flops 4663296 | bytes 7709248 | tf_op jit(solution)/shard_map/reduce_sum | solution.py:90
  103.2 1.3 collective-permute-start.17
  104.5 1.3 collective-permute-start.18
  105.8 5.0 %psum.7 = f32[3,16,128]{2,1,0:T(8,128)} all-reduce(f32[3,16,128]{2,1,0:T(8,128)S(1)} %add_multiply_fusion.3), channel_id=1, replica_groups=mesh['lon'=16,'lat'=8,'lev'=2] {'lev'}, use_global_device_ids=true, to_apply=%region_6.7 | all-reduce | flops 6144 | bytes 49152 | tf_op jit(solution)/shard_map/psum | solution.py:146
  112.3 4.2 %collective-permute-start.20 = (f32[9,8,16,2]{2,1,3,0:T(8,128)S(1)}, f32[9,8,16,2]{2,1,3,0:T(8,128)}, u32[]{:S(2)}, u32[]{:S(2)}) collective-permute-start(f32[9,8,16,2]{2,1,3,0:T(8,128)S(1)} %copy.118), channel_id=1, source_target_pairs={{16,0},{32,16},{48,32},{64,48},{80,64},{96,80},{112,96},{128,112},... | collective-permute-start | bytes 27656 | tf_op jit(solution)/shard_map/ppermute | solution.py:17
  116.5 1.9 %collective-permute-start.21 = (f32[9,8,2,128]{3,1,2,0:T(8,128)S(1)}, f32[9,8,2,128]{3,1,2,0:T(8,128)S(1)}, u32[]{:S(2)}, u32[]{:S(2)}) collective-permute-start(f32[9,8,2,128]{3,1,2,0:T(8,128)S(1)} %copy.121), channel_id=1, source_target_pairs={{0,2},{2,4},{4,6},{6,8},{8,10},{10,12},{12,14},{1,3},{3,5},{5,7},{... | collective-permute-start | bytes 221192 | tf_op jit(solution)/shard_map/ppermute | solution.py:15
  118.5 6.3 %collective-permute-start.22 = (f32[9,8,2,128]{3,1,2,0:T(8,128)S(1)}, f32[9,8,2,128]{3,1,2,0:T(8,128)S(1)}, u32[]{:S(2)}, u32[]{:S(2)}) collective-permute-start(f32[9,8,2,128]{3,1,2,0:T(8,128)S(1)} %copy.122), channel_id=1, source_target_pairs={{2,0},{4,2},{6,4},{8,6},{10,8},{12,10},{14,12},{3,1},{5,3},{7,5},{... | collective-permute-start | bytes 221192 | tf_op jit(solution)/shard_map/ppermute | solution.py:17
  125.3 1.4 %copy.120 = f32[9,8,16,2]{3,2,1,0:T(8,128)S(1)} copy(f32[9,8,16,2]{2,1,3,0:T(8,128)} %collective-permute-done.20) | data formatting | bytes 18432 | tf_op jit(solution)/shard_map/ppermute | solution.py:17
  128.8 1.6 %fusion.7 = f32[9,8,16,128]{3,2,1,0:T(8,128)} fusion(f32[9,8,19,128]{3,2,1,0:T(8,128)S(1)} %get-tuple-element.30, f32[9,8,19,128]{3,2,1,0:T(8,128)S(1)} %get-tuple-element.29, f32[9,8,16,131]{3,2,1,0:T(8,128)S(1)} %get-tuple-element.24, f32[9,8,16,131]{3,2,1,0:T(8,128)S(1)} %get-tuple-element.23, f32[8,16,128]{2,1,0:T(8,128)S(1)} %broadcast_select_fusion, ...), kind=kLoop, calls=%fused_computation.23 | loop fusion | flops 3833856 | bytes 6308128 | tf_op jit(solution)/shard_map/add | solution.py:142
  (170 shorter events, 16.9 us)
Async XLA Ops:
  0.6 17.4 %copy-start = (f32[8,9]{1,0:T(8,128)S(1)}, f32[8,9]{1,0:T(8,128)}, u32[]{:S(2)}) copy-start(f32[8,9]{1,0:T(8,128)} %param.16) | copy-start | bytes 868
  1.4 1.5 %copy-start.29 = (f32[8]{0:T(128)}, f32[8]{0:T(128)S(1)}, u32[]{:S(2)}) copy-start(f32[8]{0:T(128)S(1)} %get-tuple-element.70) | copy-start | bytes 100
  1.4 1.7 %copy-start.27 = (f32[8]{0:T(128)}, f32[8]{0:T(128)S(1)}, u32[]{:S(2)}) copy-start(f32[8]{0:T(128)S(1)} %get-tuple-element.69) | copy-start | bytes 100
  1.4 1.6 %copy-start.25 = (f32[8]{0:T(128)}, f32[8]{0:T(128)S(1)}, u32[]{:S(2)}) copy-start(f32[8]{0:T(128)S(1)} %get-tuple-element.76) | copy-start | bytes 100
  1.4 2.0 %copy-start.23 = (f32[8]{0:T(128)}, f32[8]{0:T(128)S(1)}, u32[]{:S(2)}) copy-start(f32[8]{0:T(128)S(1)} %get-tuple-element.75) | copy-start | bytes 100
  1.5 1.4 %copy-start.1 = (f32[9,8,16,128]{3,2,1,0:T(8,128)S(1)}, f32[9,8,16,128]{3,2,1,0:T(8,128)}, u32[]{:S(2)}) copy-start(f32[9,8,16,128]{3,2,1,0:T(8,128)} %param.11) | copy-start | bytes 1769476
  3.6 3.9 %copy-start.8 = (f32[8,16,128]{2,1,0:T(8,128)S(1)}, f32[8,16,128]{2,1,0:T(8,128)}, u32[]{:S(2)}) copy-start(f32[8,16,128]{2,1,0:T(8,128)} %param.14) | copy-start | bytes 196612
  3.6 7.0 %copy-start.20 = (f32[2,8,16,128]{3,2,1,0:T(8,128)S(1)}, f32[2,8,16,128]{3,2,1,0:T(8,128)}, u32[]{:S(2)}) copy-start(f32[2,8,16,128]{3,2,1,0:T(8,128)} %param.13) | copy-start | bytes 393220
  3.6 14.3 %copy-start.21 = (s32[16,128]{1,0:T(8,128)S(1)}, s32[16,128]{1,0:T(8,128)}, u32[]{:S(2)}) copy-start(s32[16,128]{1,0:T(8,128)} %param.20) | copy-start | bytes 24580
  3.6 14.4 %copy-start.34 = (s32[16]{0:T(128)S(1)}, s32[16]{0:T(128)}, u32[]{:S(2)}) copy-start(s32[16]{0:T(128)} %param.17) | copy-start | bytes 196
  3.7 14.6 %copy-start.35 = (f32[16]{0:T(128)S(1)}, f32[16]{0:T(128)}, u32[]{:S(2)}) copy-start(f32[16]{0:T(128)} %param.18) | copy-start | bytes 196
  4.4 29.2 %collective-permute-start.1 = (f32[9,1,16,128]{3,2,1,0:T(8,128)}, f32[9,1,16,128]{3,2,1,0:T(8,128)S(1)}, u32[]{:S(2)}, u32[]{:S(2)}) collective-permute-start(f32[9,1,16,128]{3,2,1,0:T(8,128)} %get-tuple-element.54), channel_id=1, source_target_pairs={{0,1},{2,3},{4,5},{6,7},{8,9},{10,11},{12,13},{14,15},{16,17},{18,... | collective-permute-start | bytes 221192 | tf_op jit(solution)/shard_map/ppermute | solution.py:15
  6.2 27.5 %collective-permute-start.2 = (f32[9,1,16,128]{3,2,1,0:T(8,128)}, f32[9,1,16,128]{3,2,1,0:T(8,128)S(1)}, u32[]{:S(2)}, u32[]{:S(2)}) collective-permute-start(f32[9,1,16,128]{3,2,1,0:T(8,128)} %get-tuple-element.55), channel_id=1, source_target_pairs={{1,0},{3,2},{5,4},{7,6},{9,8},{11,10},{13,12},{15,14},{17,16},{19,... | collective-permute-start | bytes 221192 | tf_op jit(solution)/shard_map/ppermute | solution.py:17
  7.5 10.5 %copy-start.31 = (pred[8]{0:T(512)(128)(4,1)}, pred[8]{0:T(512)(128)(4,1)S(1)}, u32[]{:S(2)}) copy-start(pred[8]{0:T(512)(128)(4,1)S(1)} %fusion.46) | copy-start | bytes 28
  7.6 21.7 %collective-permute-start = (f32[1,1,16,128]{3,2,1,0:T(8,128)S(1)}, f32[1,1,16,128]{3,2,1,0:T(8,128)S(1)}, u32[]{:S(2)}, u32[]{:S(2)}) collective-permute-start(f32[1,1,16,128]{3,2,1,0:T(8,128)S(1)} %slice.569), channel_id=1, source_target_pairs={{0,1},{2,3},{4,5},{6,7},{8,9},{10,11},{12,13},{14,15},{16,17},{18,... | collective-permute-start | bytes 24584 | tf_op jit(solution)/shard_map/ppermute | solution.py:15
  10.8 10.0 %collective-permute-start.3 = (f32[2,8,16,2]{3,2,1,0:T(8,128)S(1)}, f32[2,8,16,2]{3,2,1,0:T(8,128)S(1)}, u32[]{:S(2)}, u32[]{:S(2)}) collective-permute-start(f32[2,8,16,2]{3,2,1,0:T(8,128)S(1)} %get-tuple-element.60), channel_id=1, source_target_pairs={{0,16},{16,32},{32,48},{48,64},{64,80},{80,96},{96,112},{112,128},... | collective-permute-start | bytes 6152 | tf_op jit(solution)/shard_map/ppermute | solution.py:15
  12.5 13.3 %collective-permute-start.4 = (f32[2,8,16,2]{3,2,1,0:T(8,128)S(1)}, f32[2,8,16,2]{3,2,1,0:T(8,128)S(1)}, u32[]{:S(2)}, u32[]{:S(2)}) collective-permute-start(f32[2,8,16,2]{3,2,1,0:T(8,128)S(1)} %get-tuple-element.61), channel_id=1, source_target_pairs={{16,0},{32,16},{48,32},{64,48},{80,64},{96,80},{112,96},{128,112},... | collective-permute-start | bytes 6152 | tf_op jit(solution)/shard_map/ppermute | solution.py:17
  20.8 9.1 %collective-permute-start.7 = (f32[2,8,2,128]{3,2,1,0:T(2,128)S(1)}, f32[2,8,2,128]{3,2,1,0:T(2,128)S(1)}, u32[]{:S(2)}, u32[]{:S(2)}) collective-permute-start(f32[2,8,2,128]{3,2,1,0:T(2,128)S(1)} %get-tuple-element.62), channel_id=1, source_target_pairs={{0,2},{2,4},{4,6},{6,8},{8,10},{10,12},{12,14},{1,3},{3,5},{5,7},{... | collective-permute-start | bytes 49160 | tf_op jit(solution)/shard_map/ppermute | solution.py:15
  25.8 7.1 %collective-permute-start.8 = (f32[2,8,2,128]{3,2,1,0:T(2,128)S(1)}, f32[2,8,2,128]{3,2,1,0:T(2,128)S(1)}, u32[]{:S(2)}, u32[]{:S(2)}) collective-permute-start(f32[2,8,2,128]{3,2,1,0:T(2,128)S(1)} %get-tuple-element.63), channel_id=1, source_target_pairs={{2,0},{4,2},{6,4},{8,6},{10,8},{12,10},{14,12},{3,1},{5,3},{7,5},{... | collective-permute-start | bytes 49160 | tf_op jit(solution)/shard_map/ppermute | solution.py:17
  38.8 15.9 %collective-permute-start.5 = (f32[9,8,16,2]{2,1,3,0:T(8,128)}, f32[9,8,16,2]{2,1,3,0:T(8,128)}, u32[]{:S(2)}, u32[]{:S(2)}) collective-permute-start(f32[9,8,16,2]{2,1,3,0:T(8,128)} %copy.101), channel_id=1, source_target_pairs={{0,16},{16,32},{32,48},{48,64},{64,80},{80,96},{96,112},{112,128},... | collective-permute-start | bytes 27656 | tf_op jit(solution)/shard_map/ppermute | solution.py:15
  41.0 15.9 %collective-permute-start.6 = (f32[9,8,16,2]{2,1,3,0:T(8,128)}, f32[9,8,16,2]{2,1,3,0:T(8,128)}, u32[]{:S(2)}, u32[]{:S(2)}) collective-permute-start(f32[9,8,16,2]{2,1,3,0:T(8,128)} %copy.102), channel_id=1, source_target_pairs={{16,0},{32,16},{48,32},{64,48},{80,64},{96,80},{112,96},{128,112},... | collective-permute-start | bytes 27656 | tf_op jit(solution)/shard_map/ppermute | solution.py:17
  45.8 15.5 %collective-permute-start.9 = (f32[9,8,2,128]{3,1,2,0:T(8,128)}, f32[9,8,2,128]{3,1,2,0:T(8,128)}, u32[]{:S(2)}, u32[]{:S(2)}) collective-permute-start(f32[9,8,2,128]{3,1,2,0:T(8,128)} %copy.105), channel_id=1, source_target_pairs={{0,2},{2,4},{4,6},{6,8},{8,10},{10,12},{12,14},{1,3},{3,5},{5,7},{... | collective-permute-start | bytes 221192 | tf_op jit(solution)/shard_map/ppermute | solution.py:15
  48.5 13.8 %collective-permute-start.10 = (f32[9,8,2,128]{3,1,2,0:T(8,128)}, f32[9,8,2,128]{3,1,2,0:T(8,128)}, u32[]{:S(2)}, u32[]{:S(2)}) collective-permute-start(f32[9,8,2,128]{3,1,2,0:T(8,128)} %copy.106), channel_id=1, source_target_pairs={{2,0},{4,2},{6,4},{8,6},{10,8},{12,10},{14,12},{3,1},{5,3},{7,5},{... | collective-permute-start | bytes 221192 | tf_op jit(solution)/shard_map/ppermute | solution.py:17
  61.3 2.1 %copy-start.2 = (f32[8,19,128]{2,1,0:T(8,128)S(1)}, f32[8,19,128]{2,1,0:T(8,128)}, u32[]{:S(2)}) copy-start(f32[8,19,128]{2,1,0:T(8,128)} %get-tuple-element.58) | copy-start | bytes 233476
  61.4 2.1 %copy-start.5 = (f32[8,19,128]{2,1,0:T(8,128)S(1)}, f32[8,19,128]{2,1,0:T(8,128)}, u32[]{:S(2)}) copy-start(f32[8,19,128]{2,1,0:T(8,128)} %get-tuple-element.59) | copy-start | bytes 233476
  64.4 1.0 copy-start.28
  66.0 2.9 %copy-start.32 = (f32[9]{0:T(128)S(1)}, f32[9]{0:T(128)}, u32[]{:S(2)}) copy-start(f32[9]{0:T(128)} %param.19) | copy-start | bytes 112
  66.1 2.9 %copy-start.33 = (f32[8]{0:T(128)S(1)}, f32[8]{0:T(128)}, u32[]{:S(2)}) copy-start(f32[8]{0:T(128)} %dynamic_slice.11) | copy-start | bytes 100
  66.1 2.9 %copy-start.22 = (s32[16,128]{1,0:T(8,128)S(1)}, s32[16,128]{1,0:T(8,128)}, u32[]{:S(2)}) copy-start(s32[16,128]{1,0:T(8,128)} %param.21) | copy-start | bytes 24580
  66.3 2.7 %collective-permute-start.11 = (f32[9,1,16,128]{3,2,1,0:T(8,128)S(1)}, f32[9,1,16,128]{3,2,1,0:T(8,128)S(1)}, u32[]{:S(2)}, u32[]{:S(2)}) collective-permute-start(f32[9,1,16,128]{3,2,1,0:T(8,128)S(1)} %get-tuple-element.48), channel_id=1, source_target_pairs={{0,1},{2,3},{4,5},{6,7},{8,9},{10,11},{12,13},{14,15},{16,17},{18,... | collective-permute-start | bytes 221192 | tf_op jit(solution)/shard_map/ppermute | solution.py:15
  67.6 3.2 %collective-permute-start.12 = (f32[9,1,16,128]{3,2,1,0:T(8,128)S(1)}, f32[9,1,16,128]{3,2,1,0:T(8,128)S(1)}, u32[]{:S(2)}, u32[]{:S(2)}) collective-permute-start(f32[9,1,16,128]{3,2,1,0:T(8,128)S(1)} %get-tuple-element.49), channel_id=1, source_target_pairs={{1,0},{3,2},{5,4},{7,6},{9,8},{11,10},{13,12},{15,14},{17,16},{19,... | collective-permute-start | bytes 221192 | tf_op jit(solution)/shard_map/ppermute | solution.py:17
  69.0 3.2 %copy-start.9 = (f32[9,1,16,128]{3,2,1,0:T(8,128)}, f32[9,1,16,128]{3,2,1,0:T(8,128)S(1)}, u32[]{:S(2)}) copy-start(f32[9,1,16,128]{3,2,1,0:T(8,128)S(1)} %collective-permute-done.11) | copy-start | bytes 221188
  70.8 1.5 %copy-start.11 = (f32[9,1,16,128]{3,2,1,0:T(8,128)}, f32[9,1,16,128]{3,2,1,0:T(8,128)S(1)}, u32[]{:S(2)}) copy-start(f32[9,1,16,128]{3,2,1,0:T(8,128)S(1)} %collective-permute-done.12) | copy-start | bytes 221188
  74.4 16.1 %collective-permute-start.13 = (f32[9,8,16,2]{2,1,3,0:T(8,128)}, f32[9,8,16,2]{2,1,3,0:T(8,128)}, u32[]{:S(2)}, u32[]{:S(2)}) collective-permute-start(f32[9,8,16,2]{2,1,3,0:T(8,128)} %copy.109), channel_id=1, source_target_pairs={{0,16},{16,32},{32,48},{48,64},{64,80},{80,96},{96,112},{112,128},... | collective-permute-start | bytes 27656 | tf_op jit(solution)/shard_map/ppermute | solution.py:15
  76.6 16.1 %collective-permute-start.14 = (f32[9,8,16,2]{2,1,3,0:T(8,128)}, f32[9,8,16,2]{2,1,3,0:T(8,128)}, u32[]{:S(2)}, u32[]{:S(2)}) collective-permute-start(f32[9,8,16,2]{2,1,3,0:T(8,128)} %copy.110), channel_id=1, source_target_pairs={{16,0},{32,16},{48,32},{64,48},{80,64},{96,80},{112,96},{128,112},... | collective-permute-start | bytes 27656 | tf_op jit(solution)/shard_map/ppermute | solution.py:17
  81.4 15.8 %collective-permute-start.15 = (f32[9,8,2,128]{3,1,2,0:T(8,128)}, f32[9,8,2,128]{3,1,2,0:T(8,128)}, u32[]{:S(2)}, u32[]{:S(2)}) collective-permute-start(f32[9,8,2,128]{3,1,2,0:T(8,128)} %copy.113), channel_id=1, source_target_pairs={{0,2},{2,4},{4,6},{6,8},{8,10},{10,12},{12,14},{1,3},{3,5},{5,7},{... | collective-permute-start | bytes 221192 | tf_op jit(solution)/shard_map/ppermute | solution.py:15
  84.0 14.2 %collective-permute-start.16 = (f32[9,8,2,128]{3,1,2,0:T(8,128)}, f32[9,8,2,128]{3,1,2,0:T(8,128)}, u32[]{:S(2)}, u32[]{:S(2)}) collective-permute-start(f32[9,8,2,128]{3,1,2,0:T(8,128)} %copy.114), channel_id=1, source_target_pairs={{2,0},{4,2},{6,4},{8,6},{10,8},{12,10},{14,12},{3,1},{5,3},{7,5},{... | collective-permute-start | bytes 221192 | tf_op jit(solution)/shard_map/ppermute | solution.py:17
  97.1 2.1 %copy-start.3 = (f32[8,19,128]{2,1,0:T(8,128)S(1)}, f32[8,19,128]{2,1,0:T(8,128)}, u32[]{:S(2)}) copy-start(f32[8,19,128]{2,1,0:T(8,128)} %get-tuple-element.58) | copy-start | bytes 233476
  97.2 2.1 %copy-start.6 = (f32[8,19,128]{2,1,0:T(8,128)S(1)}, f32[8,19,128]{2,1,0:T(8,128)}, u32[]{:S(2)}) copy-start(f32[8,19,128]{2,1,0:T(8,128)} %get-tuple-element.59) | copy-start | bytes 233476
  102.1 0.9 copy-start.14
  102.1 0.9 copy-start.13
  103.2 7.6 %collective-permute-start.17 = (f32[9,1,16,128]{3,2,1,0:T(8,128)S(1)}, f32[9,1,16,128]{3,2,1,0:T(8,128)S(1)}, u32[]{:S(2)}, u32[]{:S(2)}) collective-permute-start(f32[9,1,16,128]{3,2,1,0:T(8,128)S(1)} %get-tuple-element.42), channel_id=1, source_target_pairs={{0,1},{2,3},{4,5},{6,7},{8,9},{10,11},{12,13},{14,15},{16,17},{18,... | collective-permute-start | bytes 221192 | tf_op jit(solution)/shard_map/ppermute | solution.py:15
  104.5 6.3 %collective-permute-start.18 = (f32[9,1,16,128]{3,2,1,0:T(8,128)S(1)}, f32[9,1,16,128]{3,2,1,0:T(8,128)S(1)}, u32[]{:S(2)}, u32[]{:S(2)}) collective-permute-start(f32[9,1,16,128]{3,2,1,0:T(8,128)S(1)} %get-tuple-element.43), channel_id=1, source_target_pairs={{1,0},{3,2},{5,4},{7,6},{9,8},{11,10},{13,12},{15,14},{17,16},{19,... | collective-permute-start | bytes 221192 | tf_op jit(solution)/shard_map/ppermute | solution.py:17
  111.7 13.1 %collective-permute-start.19 = (f32[9,8,16,2]{2,1,3,0:T(8,128)S(1)}, f32[9,8,16,2]{2,1,3,0:T(8,128)S(1)}, u32[]{:S(2)}, u32[]{:S(2)}) collective-permute-start(f32[9,8,16,2]{2,1,3,0:T(8,128)S(1)} %copy.117), channel_id=1, source_target_pairs={{0,16},{16,32},{32,48},{48,64},{64,80},{80,96},{96,112},{112,128},... | collective-permute-start | bytes 27656 | tf_op jit(solution)/shard_map/ppermute | solution.py:15
  112.3 13.0 %collective-permute-start.20 = (f32[9,8,16,2]{2,1,3,0:T(8,128)S(1)}, f32[9,8,16,2]{2,1,3,0:T(8,128)}, u32[]{:S(2)}, u32[]{:S(2)}) collective-permute-start(f32[9,8,16,2]{2,1,3,0:T(8,128)S(1)} %copy.118), channel_id=1, source_target_pairs={{16,0},{32,16},{48,32},{64,48},{80,64},{96,80},{112,96},{128,112},... | collective-permute-start | bytes 27656 | tf_op jit(solution)/shard_map/ppermute | solution.py:17
  116.5 11.1 %collective-permute-start.21 = (f32[9,8,2,128]{3,1,2,0:T(8,128)S(1)}, f32[9,8,2,128]{3,1,2,0:T(8,128)S(1)}, u32[]{:S(2)}, u32[]{:S(2)}) collective-permute-start(f32[9,8,2,128]{3,1,2,0:T(8,128)S(1)} %copy.121), channel_id=1, source_target_pairs={{0,2},{2,4},{4,6},{6,8},{8,10},{10,12},{12,14},{1,3},{3,5},{5,7},{... | collective-permute-start | bytes 221192 | tf_op jit(solution)/shard_map/ppermute | solution.py:15
  118.5 9.3 %collective-permute-start.22 = (f32[9,8,2,128]{3,1,2,0:T(8,128)S(1)}, f32[9,8,2,128]{3,1,2,0:T(8,128)S(1)}, u32[]{:S(2)}, u32[]{:S(2)}) collective-permute-start(f32[9,8,2,128]{3,1,2,0:T(8,128)S(1)} %copy.122), channel_id=1, source_target_pairs={{2,0},{4,2},{6,4},{8,6},{10,8},{12,10},{14,12},{3,1},{5,3},{7,5},{... | collective-permute-start | bytes 221192 | tf_op jit(solution)/shard_map/ppermute | solution.py:17
  127.7 0.9 copy-start.7
  (11 other events, 8.9 us)
where the time goes:
time: 132 us; the launch traced here: 130 us
  starting transfers between devices  63.9 us (48%)
  local copies, waits for them, and re-layouts  35.3 us (27%)
  other arithmetic  17.8 us (13%)
  waiting for transfers between devices  6.55 us (5%)
  blocking collectives  4.97 us (4%)
  between operations  1.63 us (1%)
    ppermute x11, starting transfers between devices, with_halo(): lax.ppermute(head, axis, [((i + 1) % count, i) for i in range(ends)])  44 us
    ppermute x12, starting transfers between devices, with_halo(): lax.ppermute(tail, axis, [(i, (i + 1) % count) for i in range(ends)])  19.9 us
    slice x16, local copies, waits for them, and re-layouts, with_halo(): lax.slice_in_dim(cells, cells.shape[dim] - width, cells.shape[dim], axis=...  9.57 us
    ppermute x6, local copies, waits for them, and re-layouts, with_halo(): lax.ppermute(head, axis, [((i + 1) % count, i) for i in range(ends)])  7.63 us
    ppermute x6, local copies, waits for them, and re-layouts, with_halo(): lax.ppermute(tail, axis, [(i, (i + 1) % count) for i in range(ends)])  6.89 us
    slice x6, local copies, waits for them, and re-layouts, with_halo(): head = lax.slice_in_dim(cells, 0, width, axis=dim)  6.14 us
    psum x1, blocking collectives, run_split(): emis_grad = lax.psum(emis_grad, 'lev')  4.97 us
    ppermute x11, waiting for transfers between devices, with_halo(): lax.ppermute(head, axis, [((i + 1) % count, i) for i in range(ends)])  4.71 us
  transfers between devices with their start and end apart: 23, of which 3 were waited for; matrix products, arithmetic and copies ran while one was open for 22% of the time, Pallas kernels for 0%

commit v1 on v0

--- a/solution.py
+++ b/solution.py
@@ -143,7 +143,7 @@
             + transport(lon_pad, east_pad, 3, col_count)
             + transport(lat_pad, north_pad, 2, row_count)
         )
-    emis_grad = lax.psum(emis_grad, "lev")
+    emis_grad = jnp.sum(lax.all_gather(emis_grad, "lev"), axis=0)
     return (adjoint, emis_grad)
 
 

time: 132 us -> 130 us (0.985)
  blocking collectives: 4.97 us -> 2.62 us
    psum x1 -> x0, blocking collectives: 4.97 us -> none  [run_split(): emis_grad = lax.psum(emis_grad, 'lev')]
    all_gather x0 -> x1, blocking collectives: none -> 2.62 us  [run_split(): emis_grad = jnp.sum(lax.all_gather(emis_grad, 'lev'), axis=0)]
  transfers between devices with their start and end apart: 23 -> 23, of which waited for: 3 -> 3; matrix products, arithmetic and copies ran while one was open for 22% -> 23% of each run, Pallas kernels for 0% -> 0%
where the time goes in v1:
time: 130 us; the launch traced here: 129 us
  starting transfers between devices  63.9 us (49%)
  local copies, waits for them, and re-layouts  35.3 us (27%)
  other arithmetic  18.4 us (14%)
  waiting for transfers between devices  6.55 us (5%)
  blocking collectives  2.62 us (2%)
  between operations  1.63 us (1%)
    ppermute x11, starting transfers between devices, with_halo(): lax.ppermute(head, axis, [((i + 1) % count, i) for i in range(ends)])  44 us
    ppermute x12, starting transfers between devices, with_halo(): lax.ppermute(tail, axis, [(i, (i + 1) % count) for i in range(ends)])  19.9 us
    slice x16, local copies, waits for them, and re-layouts, with_halo(): lax.slice_in_dim(cells, cells.shape[dim] - width, cells.shape[dim], axis=...  9.57 us
    ppermute x6, local copies, waits for them, and re-layouts, with_halo(): lax.ppermute(head, axis, [((i + 1) % count, i) for i in range(ends)])  7.63 us
    ppermute x6, local copies, waits for them, and re-layouts, with_halo(): lax.ppermute(tail, axis, [(i, (i + 1) % count) for i in range(ends)])  6.89 us
    slice x6, local copies, waits for them, and re-layouts, with_halo(): head = lax.slice_in_dim(cells, 0, width, axis=dim)  6.14 us
    ppermute x11, waiting for transfers between devices, with_halo(): lax.ppermute(head, axis, [((i + 1) % count, i) for i in range(ends)])  4.71 us
    concatenate x6, other arithmetic, with_halo(): jnp.concatenate([lax.ppermute(tail, axis, [(i, (i + 1) % count) for i in...  4.52 us
  transfers between devices with their start and end apart: 23, of which 3 were waited for; matrix products, arithmetic and copies ran while one was open for 23% of the time, Pallas kernels for 0%

profile of v1, /device:TPU:6, one launch (start us, length us, event | category | flops | bytes accessed | tf_op | source)
XLA Modules:
  0.0 128.6 jit_solution(3179335030440893537)
XLA Ops:
  0.7 0.8 constant_dynamic-slice_fusion
  1.5 1.4 %slice_convert_fusion = (f32[1,9,8,16,128]{4,3,2,1,0:T(8,128)S(1)}, f32[1,9,8,16,128]{4,3,2,1,0:T(8,128)S(1)}, f32[1,9,8,16,128]{4,3,2,1,0:T(8,128)S(1)}) fusion(bf16[3,9,8,16,128]{4,3,2,1,0:T(8,128)(2,1)} %param.12), kind=kLoop, calls=%fused_computation.97 | loop fusion | flops 442368 | bytes 2654208 | tf_op jit(solution)/shard_map/convert_element_type | solution.py:138
  4.4 1.7 %collective-permute-start.1 = (f32[9,1,16,128]{3,2,1,0:T(8,128)}, f32[9,1,16,128]{3,2,1,0:T(8,128)S(1)}, u32[]{:S(2)}, u32[]{:S(2)}) collective-permute-start(f32[9,1,16,128]{3,2,1,0:T(8,128)} %get-tuple-element.52), channel_id=1, source_target_pairs={{0,1},{2,3},{4,5},{6,7},{8,9},{10,11},{12,13},{14,15},{16,17},{18,... | collective-permute-start | bytes 221192 | tf_op jit(solution)/shard_map/ppermute | solution.py:15
  6.2 1.3 %collective-permute-start.2 = (f32[9,1,16,128]{3,2,1,0:T(8,128)}, f32[9,1,16,128]{3,2,1,0:T(8,128)S(1)}, u32[]{:S(2)}, u32[]{:S(2)}) collective-permute-start(f32[9,1,16,128]{3,2,1,0:T(8,128)} %get-tuple-element.53), channel_id=1, source_target_pairs={{1,0},{3,2},{5,4},{7,6},{9,8},{11,10},{13,12},{15,14},{17,16},{19,... | collective-permute-start | bytes 221192 | tf_op jit(solution)/shard_map/ppermute | solution.py:17
  7.6 3.0 %collective-permute-start = (f32[1,1,16,128]{3,2,1,0:T(8,128)S(1)}, f32[1,1,16,128]{3,2,1,0:T(8,128)S(1)}, u32[]{:S(2)}, u32[]{:S(2)}) collective-permute-start(f32[1,1,16,128]{3,2,1,0:T(8,128)S(1)} %slice.569), channel_id=1, source_target_pairs={{0,1},{2,3},{4,5},{6,7},{8,9},{10,11},{12,13},{14,15},{16,17},{18,... | collective-permute-start | bytes 24584 | tf_op jit(solution)/shard_map/ppermute | solution.py:15
  10.8 1.7 %collective-permute-start.3 = (f32[2,8,16,2]{3,2,1,0:T(8,128)S(1)}, f32[2,8,16,2]{3,2,1,0:T(8,128)S(1)}, u32[]{:S(2)}, u32[]{:S(2)}) collective-permute-start(f32[2,8,16,2]{3,2,1,0:T(8,128)S(1)} %get-tuple-element.58), channel_id=1, source_target_pairs={{0,16},{16,32},{32,48},{48,64},{64,80},{80,96},{96,112},{112,128},... | collective-permute-start | bytes 6152 | tf_op jit(solution)/shard_map/ppermute | solution.py:15
  12.5 5.4 %collective-permute-start.4 = (f32[2,8,16,2]{3,2,1,0:T(8,128)S(1)}, f32[2,8,16,2]{3,2,1,0:T(8,128)S(1)}, u32[]{:S(2)}, u32[]{:S(2)}) collective-permute-start(f32[2,8,16,2]{3,2,1,0:T(8,128)S(1)} %get-tuple-element.59), channel_id=1, source_target_pairs={{16,0},{32,16},{48,32},{64,48},{80,64},{96,80},{112,96},{128,112},... | collective-permute-start | bytes 6152 | tf_op jit(solution)/shard_map/ppermute | solution.py:17
  19.0 1.8 %collective-permute-done.3 = f32[2,8,16,2]{3,2,1,0:T(8,128)S(1)} collective-permute-done((f32[2,8,16,2]{3,2,1,0:T(8,128)S(1)}, f32[2,8,16,2]{3,2,1,0:T(8,128)S(1)}, u32[]{:S(2)}, u32[]{:S(2)}) %collective-permute-start.3) | collective-permute-done | bytes 2080 | tf_op jit(solution)/shard_map/ppermute | solution.py:15
  20.8 4.9 %collective-permute-start.7 = (f32[2,8,2,128]{3,2,1,0:T(2,128)S(1)}, f32[2,8,2,128]{3,2,1,0:T(2,128)S(1)}, u32[]{:S(2)}, u32[]{:S(2)}) collective-permute-start(f32[2,8,2,128]{3,2,1,0:T(2,128)S(1)} %get-tuple-element.60), channel_id=1, source_target_pairs={{0,2},{2,4},{4,6},{6,8},{8,10},{10,12},{12,14},{1,3},{3,5},{5,7},{... | collective-permute-start | bytes 49160 | tf_op jit(solution)/shard_map/ppermute | solution.py:15
  25.8 3.3 %collective-permute-start.8 = (f32[2,8,2,128]{3,2,1,0:T(2,128)S(1)}, f32[2,8,2,128]{3,2,1,0:T(2,128)S(1)}, u32[]{:S(2)}, u32[]{:S(2)}) collective-permute-start(f32[2,8,2,128]{3,2,1,0:T(2,128)S(1)} %get-tuple-element.61), channel_id=1, source_target_pairs={{2,0},{4,2},{6,4},{8,6},{10,8},{12,10},{14,12},{3,1},{5,3},{7,5},{... | collective-permute-start | bytes 49160 | tf_op jit(solution)/shard_map/ppermute | solution.py:17
  29.2 0.7 fusion.35
  30.0 2.9 %collective-permute-done.8 = f32[2,8,2,128]{3,2,1,0:T(2,128)S(1)} collective-permute-done((f32[2,8,2,128]{3,2,1,0:T(2,128)S(1)}, f32[2,8,2,128]{3,2,1,0:T(2,128)S(1)}, u32[]{:S(2)}, u32[]{:S(2)}) %collective-permute-start.8) | collective-permute-done | bytes 16416 | tf_op jit(solution)/shard_map/ppermute | solution.py:17
  34.3 1.1 fusion.1
  35.5 1.2 fusion.57
  36.6 2.2 %copy.101 = f32[9,8,16,2]{2,1,3,0:T(8,128)} copy(f32[9,8,16,2]{3,2,1,0:T(8,128)} %get-tuple-element.48) | data formatting | bytes 18432 | tf_op jit(solution)/shard_map/slice | solution.py:12
  38.8 2.2 %copy.102 = f32[9,8,16,2]{2,1,3,0:T(8,128)} copy(f32[9,8,16,2]{3,2,1,0:T(8,128)} %get-tuple-element.49) | data formatting | bytes 18432 | tf_op jit(solution)/shard_map/slice | solution.py:11
  41.0 4.1 %collective-permute-start.6 = (f32[9,8,16,2]{2,1,3,0:T(8,128)}, f32[9,8,16,2]{2,1,3,0:T(8,128)}, u32[]{:S(2)}, u32[]{:S(2)}) collective-permute-start(f32[9,8,16,2]{2,1,3,0:T(8,128)} %copy.102), channel_id=1, source_target_pairs={{16,0},{32,16},{48,32},{64,48},{80,64},{96,80},{112,96},{128,112},... | collective-permute-start | bytes 27656 | tf_op jit(solution)/shard_map/ppermute | solution.py:17
  45.8 2.0 %collective-permute-start.9 = (f32[9,8,2,128]{3,1,2,0:T(8,128)}, f32[9,8,2,128]{3,1,2,0:T(8,128)}, u32[]{:S(2)}, u32[]{:S(2)}) collective-permute-start(f32[9,8,2,128]{3,1,2,0:T(8,128)} %copy.105), channel_id=1, source_target_pairs={{0,2},{2,4},{4,6},{6,8},{8,10},{10,12},{12,14},{1,3},{3,5},{5,7},{... | collective-permute-start | bytes 221192 | tf_op jit(solution)/shard_map/ppermute | solution.py:15
  48.5 6.2 %collective-permute-start.10 = (f32[9,8,2,128]{3,1,2,0:T(8,128)}, f32[9,8,2,128]{3,1,2,0:T(8,128)}, u32[]{:S(2)}, u32[]{:S(2)}) collective-permute-start(f32[9,8,2,128]{3,1,2,0:T(8,128)} %copy.106), channel_id=1, source_target_pairs={{2,0},{4,2},{6,4},{8,6},{10,8},{12,10},{14,12},{3,1},{5,3},{7,5},{... | collective-permute-start | bytes 221192 | tf_op jit(solution)/shard_map/ppermute | solution.py:17
  54.7 2.2 %copy.103 = f32[9,8,16,2]{3,2,1,0:T(8,128)} copy(f32[9,8,16,2]{2,1,3,0:T(8,128)} %collective-permute-done.5) | data formatting | bytes 18432 | tf_op jit(solution)/shard_map/ppermute | solution.py:15
  56.9 2.2 %copy.104 = f32[9,8,16,2]{3,2,1,0:T(8,128)} copy(f32[9,8,16,2]{2,1,3,0:T(8,128)} %collective-permute-done.6) | data formatting | bytes 18432 | tf_op jit(solution)/shard_map/ppermute | solution.py:17
  59.1 1.8 %pad_maximum_fusion = f32[9,8,16,132]{3,2,1,0:T(8,128)S(1)} fusion(f32[9,8,16,2]{3,2,1,0:T(8,128)} %copy.104, f32[9,8,16,128]{3,2,1,0:T(8,128)S(1)} %fusion.1, f32[9,8,16,2]{3,2,1,0:T(8,128)} %copy.103), kind=kLoop, calls=%fused_computation.3 | loop fusion | flops 304128 | bytes 1216512 | tf_op jit(solution)/shard_map/concatenate | solution.py:13
  61.4 1.0 copy.107
  62.4 0.9 copy.108
  64.4 0.7 fusion.25
  66.3 1.3 %collective-permute-start.11 = (f32[9,1,16,128]{3,2,1,0:T(8,128)S(1)}, f32[9,1,16,128]{3,2,1,0:T(8,128)S(1)}, u32[]{:S(2)}, u32[]{:S(2)}) collective-permute-start(f32[9,1,16,128]{3,2,1,0:T(8,128)S(1)} %get-tuple-element.46), channel_id=1, source_target_pairs={{0,1},{2,3},{4,5},{6,7},{8,9},{10,11},{12,13},{14,15},{16,17},{18,... | collective-permute-start | bytes 221192 | tf_op jit(solution)/shard_map/ppermute | solution.py:15
  67.6 1.3 %collective-permute-start.12 = (f32[9,1,16,128]{3,2,1,0:T(8,128)S(1)}, f32[9,1,16,128]{3,2,1,0:T(8,128)S(1)}, u32[]{:S(2)}, u32[]{:S(2)}) collective-permute-start(f32[9,1,16,128]{3,2,1,0:T(8,128)S(1)} %get-tuple-element.47), channel_id=1, source_target_pairs={{1,0},{3,2},{5,4},{7,6},{9,8},{11,10},{13,12},{15,14},{17,16},{19,... | collective-permute-start | bytes 221192 | tf_op jit(solution)/shard_map/ppermute | solution.py:17
  69.0 1.7 %collective-permute-done.12 = f32[9,1,16,128]{3,2,1,0:T(8,128)S(1)} collective-permute-done((f32[9,1,16,128]{3,2,1,0:T(8,128)S(1)}, f32[9,1,16,128]{3,2,1,0:T(8,128)S(1)}, u32[]{:S(2)}, u32[]{:S(2)}) %collective-permute-start.12) | collective-permute-done | bytes 73760 | tf_op jit(solution)/shard_map/ppermute | solution.py:17
  71.0 1.2 fusion.54
  72.2 2.2 %copy.109 = f32[9,8,16,2]{2,1,3,0:T(8,128)} copy(f32[9,8,16,2]{3,2,1,0:T(8,128)} %get-tuple-element.42) | data formatting | bytes 18432 | tf_op jit(solution)/shard_map/slice | solution.py:12
  74.4 2.2 %copy.110 = f32[9,8,16,2]{2,1,3,0:T(8,128)} copy(f32[9,8,16,2]{3,2,1,0:T(8,128)} %get-tuple-element.43) | data formatting | bytes 18432 | tf_op jit(solution)/shard_map/slice | solution.py:11
  76.6 4.1 %collective-permute-start.14 = (f32[9,8,16,2]{2,1,3,0:T(8,128)}, f32[9,8,16,2]{2,1,3,0:T(8,128)}, u32[]{:S(2)}, u32[]{:S(2)}) collective-permute-start(f32[9,8,16,2]{2,1,3,0:T(8,128)} %copy.110), channel_id=1, source_target_pairs={{16,0},{32,16},{48,32},{64,48},{80,64},{96,80},{112,96},{128,112},... | collective-permute-start | bytes 27656 | tf_op jit(solution)/shard_map/ppermute | solution.py:17
  81.4 1.9 %collective-permute-start.15 = (f32[9,8,2,128]{3,1,2,0:T(8,128)}, f32[9,8,2,128]{3,1,2,0:T(8,128)}, u32[]{:S(2)}, u32[]{:S(2)}) collective-permute-start(f32[9,8,2,128]{3,1,2,0:T(8,128)} %copy.113), channel_id=1, source_target_pairs={{0,2},{2,4},{4,6},{6,8},{8,10},{10,12},{12,14},{1,3},{3,5},{5,7},{... | collective-permute-start | bytes 221192 | tf_op jit(solution)/shard_map/ppermute | solution.py:15
  84.0 6.5 %collective-permute-start.16 = (f32[9,8,2,128]{3,1,2,0:T(8,128)}, f32[9,8,2,128]{3,1,2,0:T(8,128)}, u32[]{:S(2)}, u32[]{:S(2)}) collective-permute-start(f32[9,8,2,128]{3,1,2,0:T(8,128)} %copy.114), channel_id=1, source_target_pairs={{2,0},{4,2},{6,4},{8,6},{10,8},{12,10},{14,12},{3,1},{5,3},{7,5},{... | collective-permute-start | bytes 221192 | tf_op jit(solution)/shard_map/ppermute | solution.py:17
  90.5 2.2 %copy.111 = f32[9,8,16,2]{3,2,1,0:T(8,128)} copy(f32[9,8,16,2]{2,1,3,0:T(8,128)} %collective-permute-done.13) | data formatting | bytes 18432 | tf_op jit(solution)/shard_map/ppermute | solution.py:15
  92.7 2.2 %copy.112 = f32[9,8,16,2]{3,2,1,0:T(8,128)} copy(f32[9,8,16,2]{2,1,3,0:T(8,128)} %collective-permute-done.14) | data formatting | bytes 18432 | tf_op jit(solution)/shard_map/ppermute | solution.py:17
  94.9 1.8 %pad_maximum_fusion.1 = f32[9,8,16,132]{3,2,1,0:T(8,128)S(1)} fusion(f32[9,8,16,2]{3,2,1,0:T(8,128)} %copy.112, f32[9,8,16,128]{3,2,1,0:T(8,128)S(1)} %fusion.3, f32[9,8,16,2]{3,2,1,0:T(8,128)} %copy.111), kind=kLoop, calls=%fused_computation.4 | loop fusion | flops 304128 | bytes 1216512 | tf_op jit(solution)/shard_map/concatenate | solution.py:13
  97.2 1.0 copy.115
  98.2 0.9 copy.116
  100.2 1.6 %multiply_reduce_fusion.1 = (f32[9,16,128]{2,1,0:T(8,128)}, f32[9,16,128]{2,1,0:T(8,128)}, f32[9,16,128]{2,1,0:T(8,128)}, f32[9,8,16,128]{3,2,1,0:T(8,128)S(1)}) fusion(f32[9,8,16,128]{3,2,1,0:T(8,128)S(1)} %fusion.25, f32[9,8]{1,0:T(8,128)S(1)} %broadcast_multiply_fusion.13, f32[9,8,16,128]{3,2,1,0:T(8,128)S(1)} %copy-done.1, ...), kind=kLoop, calls=%fused_computation.79 | loop fusion | flops 4663296 | bytes 7709248 | tf_op jit(solution)/shard_map/reduce_sum | solution.py:90
  103.2 1.3 %collective-permute-start.17 = (f32[9,1,16,128]{3,2,1,0:T(8,128)S(1)}, f32[9,1,16,128]{3,2,1,0:T(8,128)S(1)}, u32[]{:S(2)}, u32[]{:S(2)}) collective-permute-start(f32[9,1,16,128]{3,2,1,0:T(8,128)S(1)} %get-tuple-element.40), channel_id=1, source_target_pairs={{0,1},{2,3},{4,5},{6,7},{8,9},{10,11},{12,13},{14,15},{16,17},{18,... | collective-permute-start | bytes 221192 | tf_op jit(solution)/shard_map/ppermute | solution.py:15
  104.5 1.3 %collective-permute-start.18 = (f32[9,1,16,128]{3,2,1,0:T(8,128)S(1)}, f32[9,1,16,128]{3,2,1,0:T(8,128)S(1)}, u32[]{:S(2)}, u32[]{:S(2)}) collective-permute-start(f32[9,1,16,128]{3,2,1,0:T(8,128)S(1)} %get-tuple-element.41), channel_id=1, source_target_pairs={{1,0},{3,2},{5,4},{7,6},{9,8},{11,10},{13,12},{15,14},{17,16},{19,... | collective-permute-start | bytes 221192 | tf_op jit(solution)/shard_map/ppermute | solution.py:17
  105.8 2.6 %all_gather.4 = f32[2,3,16,128]{3,2,1,0:T(8,128)S(1)} all-gather(f32[1,3,16,128]{3,2,1,0:T(8,128)S(1)} %bitcast_multiply_fusion), channel_id=1, replica_groups=mesh['lon'=16,'lat'=8,'lev'=2] {'lev'}, dimensions={0}, use_global_device_ids=true | all-gather | bytes 73728 | tf_op jit(solution)/shard_map/all_gather | solution.py:146
  110.6 4.2 %collective-permute-start.20 = (f32[9,8,16,2]{2,1,3,0:T(8,128)S(1)}, f32[9,8,16,2]{2,1,3,0:T(8,128)}, u32[]{:S(2)}, u32[]{:S(2)}) collective-permute-start(f32[9,8,16,2]{2,1,3,0:T(8,128)S(1)} %copy.118), channel_id=1, source_target_pairs={{16,0},{32,16},{48,32},{64,48},{80,64},{96,80},{112,96},{128,112},... | collective-permute-start | bytes 27656 | tf_op jit(solution)/shard_map/ppermute | solution.py:17
  114.8 1.9 %collective-permute-start.21 = (f32[9,8,2,128]{3,1,2,0:T(8,128)S(1)}, f32[9,8,2,128]{3,1,2,0:T(8,128)S(1)}, u32[]{:S(2)}, u32[]{:S(2)}) collective-permute-start(f32[9,8,2,128]{3,1,2,0:T(8,128)S(1)} %copy.121), channel_id=1, source_target_pairs={{0,2},{2,4},{4,6},{6,8},{8,10},{10,12},{12,14},{1,3},{3,5},{5,7},{... | collective-permute-start | bytes 221192 | tf_op jit(solution)/shard_map/ppermute | solution.py:15
  116.8 6.3 %collective-permute-start.22 = (f32[9,8,2,128]{3,1,2,0:T(8,128)S(1)}, f32[9,8,2,128]{3,1,2,0:T(8,128)S(1)}, u32[]{:S(2)}, u32[]{:S(2)}) collective-permute-start(f32[9,8,2,128]{3,1,2,0:T(8,128)S(1)} %copy.122), channel_id=1, source_target_pairs={{2,0},{4,2},{6,4},{8,6},{10,8},{12,10},{14,12},{3,1},{5,3},{7,5},{... | collective-permute-start | bytes 221192 | tf_op jit(solution)/shard_map/ppermute | solution.py:17
  123.6 1.4 %copy.120 = f32[9,8,16,2]{3,2,1,0:T(8,128)S(1)} copy(f32[9,8,16,2]{2,1,3,0:T(8,128)} %collective-permute-done.20) | data formatting | bytes 18432 | tf_op jit(solution)/shard_map/ppermute | solution.py:17
  127.1 1.6 %fusion.7 = f32[9,8,16,128]{3,2,1,0:T(8,128)} fusion(f32[9,8,19,128]{3,2,1,0:T(8,128)S(1)} %get-tuple-element.28, f32[9,8,19,128]{3,2,1,0:T(8,128)S(1)} %get-tuple-element.27, f32[9,8,16,131]{3,2,1,0:T(8,128)S(1)} %get-tuple-element.22, f32[9,8,16,131]{3,2,1,0:T(8,128)S(1)} %get-tuple-element.21, f32[8,16,128]{2,1,0:T(8,128)S(1)} %broadcast_select_fusion, ...), kind=kLoop, calls=%fused_computation.23 | loop fusion | flops 3833856 | bytes 6308128 | tf_op jit(solution)/shard_map/add | solution.py:142
  (171 shorter events, 17.5 us)
Async XLA Ops:
  0.6 17.4 %copy-start = (f32[8,9]{1,0:T(8,128)S(1)}, f32[8,9]{1,0:T(8,128)}, u32[]{:S(2)}) copy-start(f32[8,9]{1,0:T(8,128)} %param.16) | copy-start | bytes 868
  1.4 1.5 %copy-start.29 = (f32[8]{0:T(128)}, f32[8]{0:T(128)S(1)}, u32[]{:S(2)}) copy-start(f32[8]{0:T(128)S(1)} %get-tuple-element.68) | copy-start | bytes 100
  1.4 1.7 %copy-start.27 = (f32[8]{0:T(128)}, f32[8]{0:T(128)S(1)}, u32[]{:S(2)}) copy-start(f32[8]{0:T(128)S(1)} %get-tuple-element.67) | copy-start | bytes 100
  1.4 1.6 %copy-start.25 = (f32[8]{0:T(128)}, f32[8]{0:T(128)S(1)}, u32[]{:S(2)}) copy-start(f32[8]{0:T(128)S(1)} %get-tuple-element.74) | copy-start | bytes 100
  1.4 2.0 %copy-start.23 = (f32[8]{0:T(128)}, f32[8]{0:T(128)S(1)}, u32[]{:S(2)}) copy-start(f32[8]{0:T(128)S(1)} %get-tuple-element.73) | copy-start | bytes 100
  1.5 1.4 %copy-start.1 = (f32[9,8,16,128]{3,2,1,0:T(8,128)S(1)}, f32[9,8,16,128]{3,2,1,0:T(8,128)}, u32[]{:S(2)}) copy-start(f32[9,8,16,128]{3,2,1,0:T(8,128)} %param.11) | copy-start | bytes 1769476
  3.6 3.9 %copy-start.8 = (f32[8,16,128]{2,1,0:T(8,128)S(1)}, f32[8,16,128]{2,1,0:T(8,128)}, u32[]{:S(2)}) copy-start(f32[8,16,128]{2,1,0:T(8,128)} %param.14) | copy-start | bytes 196612
  3.6 7.0 %copy-start.20 = (f32[2,8,16,128]{3,2,1,0:T(8,128)S(1)}, f32[2,8,16,128]{3,2,1,0:T(8,128)}, u32[]{:S(2)}) copy-start(f32[2,8,16,128]{3,2,1,0:T(8,128)} %param.13) | copy-start | bytes 393220
  3.6 14.3 %copy-start.21 = (s32[16,128]{1,0:T(8,128)S(1)}, s32[16,128]{1,0:T(8,128)}, u32[]{:S(2)}) copy-start(s32[16,128]{1,0:T(8,128)} %param.20) | copy-start | bytes 24580
  3.6 14.4 %copy-start.34 = (s32[16]{0:T(128)S(1)}, s32[16]{0:T(128)}, u32[]{:S(2)}) copy-start(s32[16]{0:T(128)} %param.17) | copy-start | bytes 196
  3.7 14.6 %copy-start.35 = (f32[16]{0:T(128)S(1)}, f32[16]{0:T(128)}, u32[]{:S(2)}) copy-start(f32[16]{0:T(128)} %param.18) | copy-start | bytes 196
  4.4 29.2 %collective-permute-start.1 = (f32[9,1,16,128]{3,2,1,0:T(8,128)}, f32[9,1,16,128]{3,2,1,0:T(8,128)S(1)}, u32[]{:S(2)}, u32[]{:S(2)}) collective-permute-start(f32[9,1,16,128]{3,2,1,0:T(8,128)} %get-tuple-element.52), channel_id=1, source_target_pairs={{0,1},{2,3},{4,5},{6,7},{8,9},{10,11},{12,13},{14,15},{16,17},{18,... | collective-permute-start | bytes 221192 | tf_op jit(solution)/shard_map/ppermute | solution.py:15
  6.2 27.5 %collective-permute-start.2 = (f32[9,1,16,128]{3,2,1,0:T(8,128)}, f32[9,1,16,128]{3,2,1,0:T(8,128)S(1)}, u32[]{:S(2)}, u32[]{:S(2)}) collective-permute-start(f32[9,1,16,128]{3,2,1,0:T(8,128)} %get-tuple-element.53), channel_id=1, source_target_pairs={{1,0},{3,2},{5,4},{7,6},{9,8},{11,10},{13,12},{15,14},{17,16},{19,... | collective-permute-start | bytes 221192 | tf_op jit(solution)/shard_map/ppermute | solution.py:17
  7.5 10.5 %copy-start.31 = (pred[8]{0:T(512)(128)(4,1)}, pred[8]{0:T(512)(128)(4,1)S(1)}, u32[]{:S(2)}) copy-start(pred[8]{0:T(512)(128)(4,1)S(1)} %fusion.46) | copy-start | bytes 28
  7.6 21.7 %collective-permute-start = (f32[1,1,16,128]{3,2,1,0:T(8,128)S(1)}, f32[1,1,16,128]{3,2,1,0:T(8,128)S(1)}, u32[]{:S(2)}, u32[]{:S(2)}) collective-permute-start(f32[1,1,16,128]{3,2,1,0:T(8,128)S(1)} %slice.569), channel_id=1, source_target_pairs={{0,1},{2,3},{4,5},{6,7},{8,9},{10,11},{12,13},{14,15},{16,17},{18,... | collective-permute-start | bytes 24584 | tf_op jit(solution)/shard_map/ppermute | solution.py:15
  10.8 10.0 %collective-permute-start.3 = (f32[2,8,16,2]{3,2,1,0:T(8,128)S(1)}, f32[2,8,16,2]{3,2,1,0:T(8,128)S(1)}, u32[]{:S(2)}, u32[]{:S(2)}) collective-permute-start(f32[2,8,16,2]{3,2,1,0:T(8,128)S(1)} %get-tuple-element.58), channel_id=1, source_target_pairs={{0,16},{16,32},{32,48},{48,64},{64,80},{80,96},{96,112},{112,128},... | collective-permute-start | bytes 6152 | tf_op jit(solution)/shard_map/ppermute | solution.py:15
  12.5 13.3 %collective-permute-start.4 = (f32[2,8,16,2]{3,2,1,0:T(8,128)S(1)}, f32[2,8,16,2]{3,2,1,0:T(8,128)S(1)}, u32[]{:S(2)}, u32[]{:S(2)}) collective-permute-start(f32[2,8,16,2]{3,2,1,0:T(8,128)S(1)} %get-tuple-element.59), channel_id=1, source_target_pairs={{16,0},{32,16},{48,32},{64,48},{80,64},{96,80},{112,96},{128,112},... | collective-permute-start | bytes 6152 | tf_op jit(solution)/shard_map/ppermute | solution.py:17
  20.8 9.1 %collective-permute-start.7 = (f32[2,8,2,128]{3,2,1,0:T(2,128)S(1)}, f32[2,8,2,128]{3,2,1,0:T(2,128)S(1)}, u32[]{:S(2)}, u32[]{:S(2)}) collective-permute-start(f32[2,8,2,128]{3,2,1,0:T(2,128)S(1)} %get-tuple-element.60), channel_id=1, source_target_pairs={{0,2},{2,4},{4,6},{6,8},{8,10},{10,12},{12,14},{1,3},{3,5},{5,7},{... | collective-permute-start | bytes 49160 | tf_op jit(solution)/shard_map/ppermute | solution.py:15
  25.8 7.1 %collective-permute-start.8 = (f32[2,8,2,128]{3,2,1,0:T(2,128)S(1)}, f32[2,8,2,128]{3,2,1,0:T(2,128)S(1)}, u32[]{:S(2)}, u32[]{:S(2)}) collective-permute-start(f32[2,8,2,128]{3,2,1,0:T(2,128)S(1)} %get-tuple-element.61), channel_id=1, source_target_pairs={{2,0},{4,2},{6,4},{8,6},{10,8},{12,10},{14,12},{3,1},{5,3},{7,5},{... | collective-permute-start | bytes 49160 | tf_op jit(solution)/shard_map/ppermute | solution.py:17
  38.8 15.9 %collective-permute-start.5 = (f32[9,8,16,2]{2,1,3,0:T(8,128)}, f32[9,8,16,2]{2,1,3,0:T(8,128)}, u32[]{:S(2)}, u32[]{:S(2)}) collective-permute-start(f32[9,8,16,2]{2,1,3,0:T(8,128)} %copy.101), channel_id=1, source_target_pairs={{0,16},{16,32},{32,48},{48,64},{64,80},{80,96},{96,112},{112,128},... | collective-permute-start | bytes 27656 | tf_op jit(solution)/shard_map/ppermute | solution.py:15
  41.0 15.9 %collective-permute-start.6 = (f32[9,8,16,2]{2,1,3,0:T(8,128)}, f32[9,8,16,2]{2,1,3,0:T(8,128)}, u32[]{:S(2)}, u32[]{:S(2)}) collective-permute-start(f32[9,8,16,2]{2,1,3,0:T(8,128)} %copy.102), channel_id=1, source_target_pairs={{16,0},{32,16},{48,32},{64,48},{80,64},{96,80},{112,96},{128,112},... | collective-permute-start | bytes 27656 | tf_op jit(solution)/shard_map/ppermute | solution.py:17
  45.8 15.5 %collective-permute-start.9 = (f32[9,8,2,128]{3,1,2,0:T(8,128)}, f32[9,8,2,128]{3,1,2,0:T(8,128)}, u32[]{:S(2)}, u32[]{:S(2)}) collective-permute-start(f32[9,8,2,128]{3,1,2,0:T(8,128)} %copy.105), channel_id=1, source_target_pairs={{0,2},{2,4},{4,6},{6,8},{8,10},{10,12},{12,14},{1,3},{3,5},{5,7},{... | collective-permute-start | bytes 221192 | tf_op jit(solution)/shard_map/ppermute | solution.py:15
  48.5 13.8 %collective-permute-start.10 = (f32[9,8,2,128]{3,1,2,0:T(8,128)}, f32[9,8,2,128]{3,1,2,0:T(8,128)}, u32[]{:S(2)}, u32[]{:S(2)}) collective-permute-start(f32[9,8,2,128]{3,1,2,0:T(8,128)} %copy.106), channel_id=1, source_target_pairs={{2,0},{4,2},{6,4},{8,6},{10,8},{12,10},{14,12},{3,1},{5,3},{7,5},{... | collective-permute-start | bytes 221192 | tf_op jit(solution)/shard_map/ppermute | solution.py:17
  61.3 2.1 %copy-start.2 = (f32[8,19,128]{2,1,0:T(8,128)S(1)}, f32[8,19,128]{2,1,0:T(8,128)}, u32[]{:S(2)}) copy-start(f32[8,19,128]{2,1,0:T(8,128)} %get-tuple-element.56) | copy-start | bytes 233476
  61.4 2.1 %copy-start.5 = (f32[8,19,128]{2,1,0:T(8,128)S(1)}, f32[8,19,128]{2,1,0:T(8,128)}, u32[]{:S(2)}) copy-start(f32[8,19,128]{2,1,0:T(8,128)} %get-tuple-element.57) | copy-start | bytes 233476
  64.4 1.0 copy-start.28
  66.0 2.9 %copy-start.32 = (f32[9]{0:T(128)S(1)}, f32[9]{0:T(128)}, u32[]{:S(2)}) copy-start(f32[9]{0:T(128)} %param.19) | copy-start | bytes 112
  66.1 2.9 %copy-start.33 = (f32[8]{0:T(128)S(1)}, f32[8]{0:T(128)}, u32[]{:S(2)}) copy-start(f32[8]{0:T(128)} %dynamic_slice.11) | copy-start | bytes 100
  66.1 2.9 %copy-start.22 = (s32[16,128]{1,0:T(8,128)S(1)}, s32[16,128]{1,0:T(8,128)}, u32[]{:S(2)}) copy-start(s32[16,128]{1,0:T(8,128)} %param.21) | copy-start | bytes 24580
  66.3 2.7 %collective-permute-start.11 = (f32[9,1,16,128]{3,2,1,0:T(8,128)S(1)}, f32[9,1,16,128]{3,2,1,0:T(8,128)S(1)}, u32[]{:S(2)}, u32[]{:S(2)}) collective-permute-start(f32[9,1,16,128]{3,2,1,0:T(8,128)S(1)} %get-tuple-element.46), channel_id=1, source_target_pairs={{0,1},{2,3},{4,5},{6,7},{8,9},{10,11},{12,13},{14,15},{16,17},{18,... | collective-permute-start | bytes 221192 | tf_op jit(solution)/shard_map/ppermute | solution.py:15
  67.6 3.2 %collective-permute-start.12 = (f32[9,1,16,128]{3,2,1,0:T(8,128)S(1)}, f32[9,1,16,128]{3,2,1,0:T(8,128)S(1)}, u32[]{:S(2)}, u32[]{:S(2)}) collective-permute-start(f32[9,1,16,128]{3,2,1,0:T(8,128)S(1)} %get-tuple-element.47), channel_id=1, source_target_pairs={{1,0},{3,2},{5,4},{7,6},{9,8},{11,10},{13,12},{15,14},{17,16},{19,... | collective-permute-start | bytes 221192 | tf_op jit(solution)/shard_map/ppermute | solution.py:17
  69.0 3.2 %copy-start.9 = (f32[9,1,16,128]{3,2,1,0:T(8,128)}, f32[9,1,16,128]{3,2,1,0:T(8,128)S(1)}, u32[]{:S(2)}) copy-start(f32[9,1,16,128]{3,2,1,0:T(8,128)S(1)} %collective-permute-done.11) | copy-start | bytes 221188
  70.8 1.5 %copy-start.11 = (f32[9,1,16,128]{3,2,1,0:T(8,128)}, f32[9,1,16,128]{3,2,1,0:T(8,128)S(1)}, u32[]{:S(2)}) copy-start(f32[9,1,16,128]{3,2,1,0:T(8,128)S(1)} %collective-permute-done.12) | copy-start | bytes 221188
  74.4 16.1 %collective-permute-start.13 = (f32[9,8,16,2]{2,1,3,0:T(8,128)}, f32[9,8,16,2]{2,1,3,0:T(8,128)}, u32[]{:S(2)}, u32[]{:S(2)}) collective-permute-start(f32[9,8,16,2]{2,1,3,0:T(8,128)} %copy.109), channel_id=1, source_target_pairs={{0,16},{16,32},{32,48},{48,64},{64,80},{80,96},{96,112},{112,128},... | collective-permute-start | bytes 27656 | tf_op jit(solution)/shard_map/ppermute | solution.py:15
  76.6 16.1 %collective-permute-start.14 = (f32[9,8,16,2]{2,1,3,0:T(8,128)}, f32[9,8,16,2]{2,1,3,0:T(8,128)}, u32[]{:S(2)}, u32[]{:S(2)}) collective-permute-start(f32[9,8,16,2]{2,1,3,0:T(8,128)} %copy.110), channel_id=1, source_target_pairs={{16,0},{32,16},{48,32},{64,48},{80,64},{96,80},{112,96},{128,112},... | collective-permute-start | bytes 27656 | tf_op jit(solution)/shard_map/ppermute | solution.py:17
  81.4 15.8 %collective-permute-start.15 = (f32[9,8,2,128]{3,1,2,0:T(8,128)}, f32[9,8,2,128]{3,1,2,0:T(8,128)}, u32[]{:S(2)}, u32[]{:S(2)}) collective-permute-start(f32[9,8,2,128]{3,1,2,0:T(8,128)} %copy.113), channel_id=1, source_target_pairs={{0,2},{2,4},{4,6},{6,8},{8,10},{10,12},{12,14},{1,3},{3,5},{5,7},{... | collective-permute-start | bytes 221192 | tf_op jit(solution)/shard_map/ppermute | solution.py:15
  84.0 14.2 %collective-permute-start.16 = (f32[9,8,2,128]{3,1,2,0:T(8,128)}, f32[9,8,2,128]{3,1,2,0:T(8,128)}, u32[]{:S(2)}, u32[]{:S(2)}) collective-permute-start(f32[9,8,2,128]{3,1,2,0:T(8,128)} %copy.114), channel_id=1, source_target_pairs={{2,0},{4,2},{6,4},{8,6},{10,8},{12,10},{14,12},{3,1},{5,3},{7,5},{... | collective-permute-start | bytes 221192 | tf_op jit(solution)/shard_map/ppermute | solution.py:17
  97.1 2.1 %copy-start.3 = (f32[8,19,128]{2,1,0:T(8,128)S(1)}, f32[8,19,128]{2,1,0:T(8,128)}, u32[]{:S(2)}) copy-start(f32[8,19,128]{2,1,0:T(8,128)} %get-tuple-element.56) | copy-start | bytes 233476
  97.2 2.1 %copy-start.6 = (f32[8,19,128]{2,1,0:T(8,128)S(1)}, f32[8,19,128]{2,1,0:T(8,128)}, u32[]{:S(2)}) copy-start(f32[8,19,128]{2,1,0:T(8,128)} %get-tuple-element.57) | copy-start | bytes 233476
  102.1 0.9 copy-start.14
  102.1 0.9 copy-start.13
  103.2 5.9 %collective-permute-start.17 = (f32[9,1,16,128]{3,2,1,0:T(8,128)S(1)}, f32[9,1,16,128]{3,2,1,0:T(8,128)S(1)}, u32[]{:S(2)}, u32[]{:S(2)}) collective-permute-start(f32[9,1,16,128]{3,2,1,0:T(8,128)S(1)} %get-tuple-element.40), channel_id=1, source_target_pairs={{0,1},{2,3},{4,5},{6,7},{8,9},{10,11},{12,13},{14,15},{16,17},{18,... | collective-permute-start | bytes 221192 | tf_op jit(solution)/shard_map/ppermute | solution.py:15
  104.5 4.6 %collective-permute-start.18 = (f32[9,1,16,128]{3,2,1,0:T(8,128)S(1)}, f32[9,1,16,128]{3,2,1,0:T(8,128)S(1)}, u32[]{:S(2)}, u32[]{:S(2)}) collective-permute-start(f32[9,1,16,128]{3,2,1,0:T(8,128)S(1)} %get-tuple-element.41), channel_id=1, source_target_pairs={{1,0},{3,2},{5,4},{7,6},{9,8},{11,10},{13,12},{15,14},{17,16},{19,... | collective-permute-start | bytes 221192 | tf_op jit(solution)/shard_map/ppermute | solution.py:17
  110.0 13.1 %collective-permute-start.19 = (f32[9,8,16,2]{2,1,3,0:T(8,128)S(1)}, f32[9,8,16,2]{2,1,3,0:T(8,128)S(1)}, u32[]{:S(2)}, u32[]{:S(2)}) collective-permute-start(f32[9,8,16,2]{2,1,3,0:T(8,128)S(1)} %copy.117), channel_id=1, source_target_pairs={{0,16},{16,32},{32,48},{48,64},{64,80},{80,96},{96,112},{112,128},... | collective-permute-start | bytes 27656 | tf_op jit(solution)/shard_map/ppermute | solution.py:15
  110.6 13.0 %collective-permute-start.20 = (f32[9,8,16,2]{2,1,3,0:T(8,128)S(1)}, f32[9,8,16,2]{2,1,3,0:T(8,128)}, u32[]{:S(2)}, u32[]{:S(2)}) collective-permute-start(f32[9,8,16,2]{2,1,3,0:T(8,128)S(1)} %copy.118), channel_id=1, source_target_pairs={{16,0},{32,16},{48,32},{64,48},{80,64},{96,80},{112,96},{128,112},... | collective-permute-start | bytes 27656 | tf_op jit(solution)/shard_map/ppermute | solution.py:17
  114.8 11.1 %collective-permute-start.21 = (f32[9,8,2,128]{3,1,2,0:T(8,128)S(1)}, f32[9,8,2,128]{3,1,2,0:T(8,128)S(1)}, u32[]{:S(2)}, u32[]{:S(2)}) collective-permute-start(f32[9,8,2,128]{3,1,2,0:T(8,128)S(1)} %copy.121), channel_id=1, source_target_pairs={{0,2},{2,4},{4,6},{6,8},{8,10},{10,12},{12,14},{1,3},{3,5},{5,7},{... | collective-permute-start | bytes 221192 | tf_op jit(solution)/shard_map/ppermute | solution.py:15
  116.8 9.3 %collective-permute-start.22 = (f32[9,8,2,128]{3,1,2,0:T(8,128)S(1)}, f32[9,8,2,128]{3,1,2,0:T(8,128)S(1)}, u32[]{:S(2)}, u32[]{:S(2)}) collective-permute-start(f32[9,8,2,128]{3,1,2,0:T(8,128)S(1)} %copy.122), channel_id=1, source_target_pairs={{2,0},{4,2},{6,4},{8,6},{10,8},{12,10},{14,12},{3,1},{5,3},{7,5},{... | collective-permute-start | bytes 221192 | tf_op jit(solution)/shard_map/ppermute | solution.py:17
  125.9 0.9 copy-start.7
  (11 other events, 8.9 us)
